TPU v7x, 256 devices: a whole 4x4x8 slice. The times are simulated.
256 devices in a mesh: rows: 16 (over x, z_hi, core), params: 16 (over z_lo, y).
Axes of the slice: x: 4, y: 4, z: 8 (z_hi: 2, z_lo: 4; z = z_hi * 4 + z_lo), core: 2. Of those that a mesh axis runs over, the one named last changes fastest.
Arguments:
- jacobian: bfloat16 [32768, 12288], P('rows', 'params'), may hold values from -0.0546875 to 0.0546875
- pattern: int32 [256, 96], P('rows', 'params'), may hold values from 0 to 1, as said below
- row_class: int32 [32768], P('rows'), may hold values from 0 to 15
- class_weight: float32 [16], replicated, may hold values from 0.1 to 10
- probes: bfloat16 [32, 12288], P(None, 'params'), may hold values from -6 to 6
Outputs:
- basis: bfloat16 [32, 12288], P(None, 'params')
Inputs may be any that keep to these rules, and one draw needn't show every extreme that they name: `pattern`: 1 marks a nonzero block of the Jacobian, 0 a zero block.
All inputs are finite; a program needn't handle non-finite values.
Results may differ from a plain program's by a relative error of at most 0.0075.
Values may be sent and summed in bfloat16 or wider, within the bound.
A program may use at most 64 MiB of HBM per device.

v0:
```python
import math

import jax
import jax.numpy as jnp
from jax import lax
from jax.sharding import PartitionSpec as P

P_SIZE = 12288
ITERS = 4


def local(jacobian, pattern, row_class, class_weight, probes):
    block = jacobian.shape[0] // pattern.shape[0]
    mask_full = jnp.repeat(jnp.repeat(pattern, block, axis=0), block, axis=1)
    masked = jacobian * mask_full.astype(jnp.bfloat16)
    classes = jnp.arange(class_weight.shape[0], dtype=jnp.int32)
    onehot = (row_class[None, :] == classes[:, None]).astype(jnp.float32)
    weight = jnp.sum(onehot * class_weight[:, None], axis=0)
    scale = math.sqrt(P_SIZE)
    basis = probes
    for step in range(ITERS):
        zpart = lax.dot_general(
            basis, masked, (((1,), (1,)), ((), ())), preferred_element_type=jnp.float32
        )
        ztotal = lax.psum(zpart, "params")
        weighted = (ztotal * weight[None, :]).astype(jnp.bfloat16)
        ypart = jnp.dot(weighted, masked, preferred_element_type=jnp.float32)
        ytotal = lax.psum(ypart, "rows")
        gram = lax.psum(jnp.dot(ytotal, ytotal.T, precision=lax.Precision.HIGHEST), "params")
        lower = jnp.linalg.cholesky(gram)
        solved = lax.linalg.triangular_solve(lower, ytotal, left_side=True, lower=True)
        basis = (solved * scale).astype(jnp.bfloat16)
    return basis


def solution(mesh):
    placed = (P("rows", "params"), P("rows", "params"), P("rows"), P(), P(None, "params"))
    return jax.shard_map(
        local, mesh=mesh, in_specs=placed, out_specs=P(None, "params"), check_vma=False
    )
```

profile of v0, /device:TPU:1, one launch (start us, length us, event | category | flops | bytes accessed | tf_op | source)
XLA Modules:
  0.0 1679.0 jit_solution(16454283900543719052)
XLA Ops:
  7.3 4.8 copy.24
  12.1 2.1 bitcast_multiply_fusion
  14.3 1.4 convolution_bitcast_fusion
  15.8 155.1 %all-reduce.9.cloned.1.call-done = f32[32,2048]{1,0:T(8,128)} async-done(((f32[32,2048]{1,0:T(8,128)}), f32[32,2048]{1,0:T(8,128)}) %all-reduce.9.cloned.1.call-update) | async-done | bytes 262160 | tf_op jit(solution)/shard_map/psum | solution.py:25
  170.9 2.6 fusion.4
  173.6 178.9 %all-reduce.11.cloned.1.call-done = f32[32,768]{1,0:T(8,128)} async-done(((f32[32,768]{1,0:T(8,128)}), f32[32,768]{1,0:T(8,128)}) %all-reduce.11.cloned.1.call-update) | async-done | bytes 98320 | tf_op jit(solution)/shard_map/psum | solution.py:28
  353.7 63.2 %psum.86 = f32[32,32]{0,1:T(8,128)S(1)} all-reduce(f32[32,32]{0,1:T(8,128)S(1)} %fusion.30), channel_id=1, replica_groups=mesh['rows'=16,'params'=16] {'params'}, use_global_device_ids=true, to_apply=%region_3.0 | all-reduce | flops 1024 | bytes 8192 | tf_op jit(solution)/shard_map/psum | solution.py:29
  417.0 2.9 cholesky.74
  421.2 2.4 custom-call.8
  424.9 1.4 fusion.31
  426.3 160.2 %all-reduce.13.cloned.1.call-done = f32[32,2048]{1,0:T(8,128)} async-done(((f32[32,2048]{1,0:T(8,128)}), f32[32,2048]{1,0:T(8,128)}) %all-reduce.13.cloned.1.call-update) | async-done | bytes 262160 | tf_op jit(solution)/shard_map/psum | solution.py:25
  586.5 2.6 fusion.5
  589.2 178.9 %all-reduce.15.cloned.1.call-done = f32[32,768]{1,0:T(8,128)} async-done(((f32[32,768]{1,0:T(8,128)}), f32[32,768]{1,0:T(8,128)}) %all-reduce.15.cloned.1.call-update) | async-done | bytes 98320 | tf_op jit(solution)/shard_map/psum | solution.py:28
  769.3 63.2 %psum.89 = f32[32,32]{0,1:T(8,128)S(1)} all-reduce(f32[32,32]{0,1:T(8,128)S(1)} %fusion.32), channel_id=1, replica_groups=mesh['rows'=16,'params'=16] {'params'}, use_global_device_ids=true, to_apply=%region_8.11 | all-reduce | flops 1024 | bytes 8192 | tf_op jit(solution)/shard_map/psum | solution.py:29
  832.5 2.9 cholesky.85
  836.8 2.4 custom-call.9
  839.2 1.2 fusion.1
  840.4 1.4 fusion.33
  841.8 160.2 %all-reduce.17.cloned.1.call-done = f32[32,2048]{1,0:T(8,128)} async-done(((f32[32,2048]{1,0:T(8,128)}), f32[32,2048]{1,0:T(8,128)}) %all-reduce.17.cloned.1.call-update) | async-done | bytes 262160 | tf_op jit(solution)/shard_map/psum | solution.py:25
  1002.0 2.6 fusion.6
  1004.7 178.9 %all-reduce.19.cloned.1.call-done = f32[32,768]{1,0:T(8,128)} async-done(((f32[32,768]{1,0:T(8,128)}), f32[32,768]{1,0:T(8,128)}) %all-reduce.19.cloned.1.call-update) | async-done | bytes 98320 | tf_op jit(solution)/shard_map/psum | solution.py:28
  1184.8 63.1 %psum.92 = f32[32,32]{0,1:T(8,128)S(1)} all-reduce(f32[32,32]{0,1:T(8,128)S(1)} %fusion.34), channel_id=1, replica_groups=mesh['rows'=16,'params'=16] {'params'}, use_global_device_ids=true, to_apply=%region_11.14 | all-reduce | flops 1024 | bytes 8192 | tf_op jit(solution)/shard_map/psum | solution.py:29
  1248.1 2.9 cholesky.96
  1252.3 2.4 custom-call.10
  1256.0 1.4 fusion.35
  1257.4 160.2 %all-reduce.21.cloned.1.call-done = f32[32,2048]{1,0:T(8,128)} async-done(((f32[32,2048]{1,0:T(8,128)}), f32[32,2048]{1,0:T(8,128)}) %all-reduce.21.cloned.1.call-update) | async-done | bytes 262160 | tf_op jit(solution)/shard_map/psum | solution.py:25
  1417.6 2.6 fusion.7
  1420.2 179.0 %all-reduce.23.cloned.1.call-done = f32[32,768]{1,0:T(8,128)} async-done(((f32[32,768]{1,0:T(8,128)}), f32[32,768]{1,0:T(8,128)}) %all-reduce.23.cloned.1.call-update) | async-done | bytes 98320 | tf_op jit(solution)/shard_map/psum | solution.py:28
  1600.4 63.2 %psum.95 = f32[32,32]{0,1:T(8,128)S(1)} all-reduce(f32[32,32]{0,1:T(8,128)S(1)} %fusion.36), channel_id=1, replica_groups=mesh['rows'=16,'params'=16] {'params'}, use_global_device_ids=true, to_apply=%region_14.17 | all-reduce | flops 1024 | bytes 8192 | tf_op jit(solution)/shard_map/psum | solution.py:29
  1663.6 2.9 cholesky.107
  1667.9 2.4 custom-call.11
  1670.3 1.8 fusion.3
  (52 shorter events, 14.1 us)
Async XLA Ops:
  6.5 7.7 copy-start
  6.5 164.4 %all-reduce.9.cloned.1.call-start = ((), (), s32[]{:S(2)}) async-start(), calls=%async_computation | async-start | bytes 524288 | tf_op jit(solution)/shard_map/psum | solution.py:25
  14.2 1.5 copy-start.1
  14.2 1.4 copy-start.2
  15.6 336.9 %all-reduce.11.cloned.1.call-start = ((), (), s32[]{:S(2)}) async-start(), calls=%async_computation.1 | async-start | bytes 196608 | tf_op jit(solution)/shard_map/psum | solution.py:28
  173.6 412.9 %all-reduce.13.cloned.1.call-start = ((), (), s32[]{:S(2)}) async-start(), calls=%async_computation.2 | async-start | bytes 524288 | tf_op jit(solution)/shard_map/psum | solution.py:25
  426.3 341.8 %all-reduce.15.cloned.1.call-start = ((), (), s32[]{:S(2)}) async-start(), calls=%async_computation.3 | async-start | bytes 196608 | tf_op jit(solution)/shard_map/psum | solution.py:28
  589.1 412.9 %all-reduce.17.cloned.1.call-start = ((), (), s32[]{:S(2)}) async-start(), calls=%async_computation.4 | async-start | bytes 524288 | tf_op jit(solution)/shard_map/psum | solution.py:25
  841.8 341.9 %all-reduce.19.cloned.1.call-start = ((), (), s32[]{:S(2)}) async-start(), calls=%async_computation.5 | async-start | bytes 196608 | tf_op jit(solution)/shard_map/psum | solution.py:28
  1004.7 412.9 %all-reduce.21.cloned.1.call-start = ((), (), s32[]{:S(2)}) async-start(), calls=%async_computation.6 | async-start | bytes 524288 | tf_op jit(solution)/shard_map/psum | solution.py:25
  1257.4 341.8 %all-reduce.23.cloned.1.call-start = ((), (), s32[]{:S(2)}) async-start(), calls=%async_computation.7 | async-start | bytes 196608 | tf_op jit(solution)/shard_map/psum | solution.py:28
Sparse Core Ops, SparseCore 0:
  15.8 155.1 all-reduce.8
  173.7 178.7 all-reduce.10
  426.4 160.0 all-reduce.12
  589.3 178.7 all-reduce.14
  841.9 160.0 all-reduce.16
  1004.8 178.8 all-reduce.18
  1257.5 160.0 all-reduce.20
  1420.3 178.7 all-reduce.22
where the time goes:
time: 1700 us; the launch traced here: 1680 us
  waiting for transfers between devices  1350 us (79%)
  blocking collectives  253 us (15%)
  other arithmetic  29.7 us (2%)
  matrix products  26.1 us (2%)
    psum x4, waiting for transfers between devices, local(): ytotal = lax.psum(ypart, 'rows')  716 us
    psum x4, waiting for transfers between devices, local(): ztotal = lax.psum(zpart, 'params')  636 us
    psum x4, blocking collectives, local(): lax.psum(jnp.dot(ytotal, ytotal.T, precision=lax.Precision.HIGHEST), 'par...  253 us
  transfers between devices with their start and end apart: 8, of which 8 were waited for; matrix products, arithmetic and copies ran while one was open for 0% of the time, Pallas kernels for 0%

commit v1 on v0

v1 whole, which is shorter than its diff:
```python
import functools
import math

import jax
import jax.numpy as jnp
from jax import lax
from jax.experimental import pallas as pl
from jax.experimental.pallas import tpu as pltpu
from jax.sharding import PartitionSpec as P

P_SIZE = 12288
BLOCK = 128
ITERS = 4
NY, NZ, NX = 4, 4, 4
MESH = pl.DeviceIdType.MESH
BF16, F32 = jnp.bfloat16, jnp.float32


def dot_t(a, b):
    return lax.dot_general(a, b, (((1,), (1,)), ((), ())), preferred_element_type=F32)


def dot(a, b):
    return jnp.dot(a, b, preferred_element_type=F32)


def pack_gram(g):
    return g[0:8] + pltpu.roll(g[8:16], 32, 1) + pltpu.roll(g[16:24], 64, 1) + pltpu.roll(g[24:32], 96, 1)


def scaled_inverse(gp, scale):
    a = jnp.concatenate([gp, pltpu.roll(gp, 96, 1), pltpu.roll(gp, 64, 1), pltpu.roll(gp, 32, 1)], axis=0)
    n = a.shape[0]
    row = lax.broadcasted_iota(jnp.int32, a.shape, 0)
    lane = lax.broadcasted_iota(jnp.int32, a.shape, 1)
    b = jnp.where(lane < n, a, jnp.where(lane - n == row, 1.0, 0.0))
    for j in range(n - 1):
        factor = b[:, j : j + 1] * (1.0 / b[j : j + 1, j : j + 1])
        b = jnp.where(row > j, b - factor * b[j : j + 1, :], b)
    diag = jnp.sum(jnp.where(lane == row, b, 0.0), axis=1, keepdims=True)
    inv = pltpu.roll(b, 128 - n, 1) * (lax.rsqrt(diag) * scale)
    return inv[:, :n]


def kernel(pattern, class_weight, jac, row_class, probes, out, m, w, w16, qpad, yacc,
           za_s, za_r, zb, zc, ga, gb, ya_s, ya_r, yb, yc, yd, load_sem,
           za_ss, za_rs, zb_ss, zb_rs, zc_ss, zc_rs, ga_ss, ga_rs, gb_ss, gb_rs,
           ya_ss, ya_rs, yb_ss, yb_rs, yc_ss, yc_rs, yd_ss, yd_rs):
    rows, params = lax.axis_index("rows"), lax.axis_index("params")
    y, zl = lax.rem(params, NY), lax.div(params, NY)
    core, zh, x = lax.rem(rows, 2), lax.rem(lax.div(rows, 2), 2), lax.div(rows, 4)
    chunk = m.shape[0] // NY
    scale = math.sqrt(P_SIZE)
    pending = []

    y_peer = [{"params": zl * NY + lax.rem(y + d, NY)} for d in range(NY)]
    z_peer = [{"params": lax.rem(zl + d, NZ) * NY + y} for d in range(NZ)]
    x_peer = [{"rows": lax.rem(x + d, NX) * 4 + zh * 2 + core} for d in range(NX)]
    zh_peer = {"rows": x * 4 + (1 - zh) * 2 + core}
    core_peer = {"rows": x * 4 + zh * 2 + (1 - core)}

    def send(src, dst, ssem, rsem, peer):
        copy = pltpu.make_async_remote_copy(
            src_ref=src, dst_ref=dst, send_sem=ssem, recv_sem=rsem, device_id=peer, device_id_type=MESH)
        copy.start()
        pending.append(copy)
        return copy

    loads = []
    for c in range(NY):
        copy = pltpu.make_async_copy(
            jac.at[pl.ds(c * chunk, chunk), :], m.at[pl.ds(c * chunk, chunk), :], load_sem.at[c])
        copy.start()
        loads.append(copy)

    barrier = pltpu.get_barrier_semaphore()
    friends = y_peer[1:] + z_peer[1:] + x_peer[1:] + [zh_peer, core_peer]
    for peer in friends:
        pl.semaphore_signal(barrier, inc=1, device_id=peer, device_id_type=MESH)

    classes = row_class[...]
    weight = jnp.zeros(classes.shape, F32)
    for c in range(class_weight.shape[0]):
        weight = jnp.where(classes == c, class_weight[c], weight)
    w16[...] = weight
    per = chunk // BLOCK
    for c in range(NY):
        for i in range(per):
            w[c, :, i * BLOCK : (i + 1) * BLOCK] = w16[c * per + i : c * per + i + 1, :]
    qpad[...] = jnp.zeros_like(qpad)

    for c in range(NY):
        loads[c].wait()
        for i in range(per):
            r = c * per + i
            for j in range(pattern.shape[1]):
                keep = jnp.full((BLOCK, BLOCK), pattern[r, j].astype(F32)).astype(BF16)
                at = (pl.ds(r * BLOCK, BLOCK), pl.ds(j * BLOCK, BLOCK))
                m[at] = m[at] * keep

    pl.semaphore_wait(barrier, len(friends))

    def rows_of(c):
        return m[pl.ds(pl.multiple_of(c * chunk, chunk), chunk), :]

    def send_gram(k, q):
        qpad[0:32, :] = q
        ga[k, y] = pack_gram(dot_t(q, qpad[...]))
        return [send(ga.at[k, y], ga.at[k, y], ga_ss.at[k, d - 1], ga_rs.at[k, d - 1], y_peer[d])
                for d in (2, 1, 3)]

    def forward_gram(k, copies):
        for copy in copies:
            copy.wait_recv()
        gb[k, zl] = ((ga[k, 0] + ga[k, 1]) + ga[k, 2]) + ga[k, 3]
        return [send(gb.at[k, zl], gb.at[k, zl], gb_ss.at[k, d - 1], gb_rs.at[k, d - 1], z_peer[d])
                for d in (1, 2, 3)]

    def finish_gram(k, copies):
        for copy in copies:
            copy.wait_recv()
        inv = scaled_inverse(((gb[k, 0] + gb[k, 1]) + gb[k, 2]) + gb[k, 3], scale)
        high = inv.astype(BF16)
        low = (inv - high.astype(F32)).astype(BF16)
        return jnp.concatenate([high, low], axis=0)

    def apply(inv2, v):
        u = dot(inv2, v)
        return u[:32] + u[32:]

    q = probes[...]
    for k in range(ITERS):
        a_copies = {}
        for d in (2, 1, 3):
            za_s[k, d - 1] = dot_t(q, rows_of(lax.rem(y + d, NY))).astype(BF16)
            a_copies[d] = send(za_s.at[k, d - 1], za_r.at[k, d - 1], za_ss.at[k, d - 1], za_rs.at[k, d - 1], y_peer[d])
        if k > 0:
            g_copies = send_gram(k - 1, q)
        own = dot_t(q, rows_of(y))
        for d in (1, 3, 2):
            a_copies[d].wait_recv()
            own = own + za_r[k, d - 1].astype(F32)
        zb[k, zl] = own.astype(BF16)
        b_copies = [send(zb.at[k, zl], zb.at[k, zl], zb_ss.at[k, d - 1], zb_rs.at[k, d - 1], z_peer[d])
                    for d in (1, 2, 3)]
        if k > 0:
            g_copies = forward_gram(k - 1, g_copies)
        for copy in b_copies:
            copy.wait_recv()
        total = ((zb[k, 0].astype(F32) + zb[k, 1].astype(F32)) + zb[k, 2].astype(F32)) + zb[k, 3].astype(F32)
        zc[k, y] = total.astype(BF16)
        c_copies = {d: send(zc.at[k, y], zc.at[k, y], zc_ss.at[k, d - 1], zc_rs.at[k, d - 1], y_peer[d])
                    for d in (2, 1, 3)}
        if k > 0:
            inv2 = finish_gram(k - 1, g_copies)
        acc = None
        for d in (0, 1, 3, 2):
            c = lax.rem(y + NY - d, NY)
            if d:
                c_copies[d].wait_recv()
            z = zc[k, c]
            z = z.astype(F32) if k == 0 else apply(inv2, z)
            v = (z * w[c]).astype(BF16)
            part = dot(v, rows_of(c))
            acc = part if acc is None else acc + part
        yacc[0] = acc[:16]
        yacc[1] = acc[16:]
        ya_s[k] = yacc[1 - core].astype(BF16)
        copy = send(ya_s.at[k], ya_r.at[k], ya_ss.at[k], ya_rs.at[k], core_peer)
        copy.wait_recv()
        yb[k, 0] = (yacc[core] + ya_r[k].astype(F32)).astype(BF16)
        copy = send(yb.at[k, 0], yb.at[k, 1], yb_ss.at[k], yb_rs.at[k], zh_peer)
        copy.wait_recv()
        yc[k, x] = (yb[k, 0].astype(F32) + yb[k, 1].astype(F32)).astype(BF16)
        copies = [send(yc.at[k, x], yc.at[k, x], yc_ss.at[k, d - 1], yc_rs.at[k, d - 1], x_peer[d])
                  for d in (2, 1, 3)]
        for copy in copies:
            copy.wait_recv()
        total = ((yc[k, 0].astype(F32) + yc[k, 1].astype(F32)) + yc[k, 2].astype(F32)) + yc[k, 3].astype(F32)
        yd[k, core] = total.astype(BF16)
        copy = send(yd.at[k, core], yd.at[k, core], yd_ss.at[k], yd_rs.at[k], core_peer)
        copy.wait_recv()
        q = jnp.concatenate([yd[k, 0], yd[k, 1]], axis=0)

    g_copies = forward_gram(ITERS - 1, send_gram(ITERS - 1, q))
    inv2 = finish_gram(ITERS - 1, g_copies)
    out[...] = apply(inv2, q).astype(BF16)
    for copy in pending:
        copy.wait_send()


def local(jacobian, pattern, row_class, class_weight, probes):
    nrows, ncols = jacobian.shape
    chunk = nrows // NY
    k = ITERS
    vmem, dma = pltpu.VMEM, pltpu.SemaphoreType.DMA
    return pl.pallas_call(
        kernel,
        out_shape=jax.ShapeDtypeStruct(probes.shape, BF16),
        in_specs=[
            pl.BlockSpec(memory_space=pltpu.SMEM),
            pl.BlockSpec(memory_space=pltpu.SMEM),
            pl.BlockSpec(memory_space=pl.ANY),
            pl.BlockSpec(memory_space=pltpu.VMEM),
            pl.BlockSpec(memory_space=pltpu.VMEM),
        ],
        out_specs=pl.BlockSpec(memory_space=pltpu.VMEM),
        scratch_shapes=[
            vmem((nrows, ncols), BF16), vmem((NY, 1, chunk), F32), vmem((nrows // 128, 128), F32),
            vmem((128, ncols), BF16), vmem((2, 16, ncols), F32),
            vmem((k, 3, 32, chunk), BF16), vmem((k, 3, 32, chunk), BF16),
            vmem((k, NZ, 32, chunk), BF16), vmem((k, NY, 32, chunk), BF16),
            vmem((k, NY, 8, 128), F32), vmem((k, NZ, 8, 128), F32),
            vmem((k, 16, ncols), BF16), vmem((k, 16, ncols), BF16),
            vmem((k, 2, 16, ncols), BF16), vmem((k, NX, 16, ncols), BF16), vmem((k, 2, 16, ncols), BF16),
            dma((NY,)),
            dma((k, 3)), dma((k, 3)), dma((k, 3)), dma((k, 3)), dma((k, 3)), dma((k, 3)),
            dma((k, 3)), dma((k, 3)), dma((k, 3)), dma((k, 3)),
            dma((k,)), dma((k,)), dma((k,)), dma((k,)), dma((k, 3)), dma((k, 3)), dma((k,)), dma((k,)),
        ],
        compiler_params=pltpu.CompilerParams(collective_id=0, has_side_effects=True),
    )(pattern, class_weight, jacobian, row_class.reshape(-1, 128), probes)


def solution(mesh):
    placed = (P("rows", "params"), P("rows", "params"), P("rows"), P(), P(None, "params"))
    return jax.shard_map(
        local, mesh=mesh, in_specs=placed, out_specs=P(None, "params"), check_vma=False
    )
```

time: 1700 us -> 120 us (0.07); the launches traced: 1680 us -> 119 us
  waiting for transfers between devices: 1350 us -> 0 us
  blocking collectives: 253 us -> 0 us
  Pallas kernels: 0 us -> 117 us
  other arithmetic: 29.7 us -> 0 us
  matrix products: 26.1 us -> 0 us
    psum x8 -> x0, waiting for transfers between devices: 1350 us -> none  [the longest x4 716 us: local(): ytotal = lax.psum(ypart, 'rows')]
    psum x4 -> x0, blocking collectives: 253 us -> none  [local(): lax.psum(jnp.dot(ytotal, ytotal.T, precision=lax.Precision.HIGHEST), 'par...]
    pallas_call x0 -> x1, Pallas kernels: none -> 117 us  [local(): pl.pallas_call(kernel, out_shape=jax.ShapeDtypeStruct(probes.shape, BF16)...]
    another operation x20 -> x0, other arithmetic: 26.7 us -> none  [the longest x12 14.4 us: local(): lower = jnp.linalg.cholesky(gram)]
    dot_general x12 -> x0, matrix products: 20.7 us -> none  [the longest x4 10.5 us: local(): ypart = jnp.dot(weighted, masked, preferred_element_type=jnp.float32)]
  transfers between devices with their start and end apart: 8 -> 0, of which waited for: 8 -> 0; matrix products, arithmetic and copies ran while one was open for 0% -> 0% of each run, Pallas kernels for 0% -> 0%
where the time goes in v1:
time: 120 us; the launch traced here: 119 us
  Pallas kernels  117 us (98%)
  local copies, waits for them, and re-layouts  2.78 us (2%)
    pallas_call x1, Pallas kernels, local(): pl.pallas_call(kernel, out_shape=jax.ShapeDtypeStruct(probes.shape, BF16)...  117 us
    unnamed x2, local copies, waits for them, and re-layouts  2.78 us

profile of v1, /device:TPU:1, one launch (start us, length us, event | category | flops | bytes accessed | tf_op | source)
XLA Modules:
  0.0 119.4 jit_solution(16226402990384818210)
XLA Ops:
  0.0 1.4 %copy.6.pattern = s32[16,6]{1,0:T(8,128)} copy(s32[16,6]{0,1:T(8,128)} %param.6) | data formatting | bytes 768 | tf_op args[1]
  1.4 116.6 %shard_map.55 = bf16[32,768]{1,0:T(8,128)(2,1)} custom-call(s32[16,6]{1,0:T(8,128)} %copy.6.pattern, f32[16]{0:T(128)} %class_weight.1, bf16[2048,768]{1,0:T(8,128)(2,1)} %jac.1, s32[16,128]{1,0:T(8,128)} %bitcast.1, bf16[32,768]{1,0:T(8,128)(2,1)} %probes.1), custom_call_target="tpu_custom_call" | custom-call | tf_op jit(solution)/shard_map/pallas_call | solution.py:197
  118.0 1.4 %copy.8 = bf16[32,768]{1,0:T(8,128)(2,1)} copy(bf16[32,768]{1,0:T(8,128)(2,1)} %shard_map.55) | data formatting | bytes 98304

commit v2 on v1

v2 whole, which is shorter than its diff:
```python
import functools
import math

import jax
import jax.numpy as jnp
from jax import lax
from jax.experimental import pallas as pl
from jax.experimental.pallas import tpu as pltpu
from jax.sharding import PartitionSpec as P

P_SIZE = 12288
BLOCK = 128
ITERS = 4
NY, NZ, NX = 4, 4, 4
MESH = pl.DeviceIdType.MESH
BF16, F32 = jnp.bfloat16, jnp.float32


def dot_t(a, b):
    return lax.dot_general(a, b, (((1,), (1,)), ((), ())), preferred_element_type=F32)


def dot(a, b):
    return jnp.dot(a, b, preferred_element_type=F32)


def pack_gram(g):
    return g[0:8] + pltpu.roll(g[8:16], 32, 1) + pltpu.roll(g[16:24], 64, 1) + pltpu.roll(g[24:32], 96, 1)


def scaled_inverse(gp, scale):
    a = jnp.concatenate([gp, pltpu.roll(gp, 96, 1), pltpu.roll(gp, 64, 1), pltpu.roll(gp, 32, 1)], axis=0)
    n = a.shape[0]
    row = lax.broadcasted_iota(jnp.int32, a.shape, 0)
    lane = lax.broadcasted_iota(jnp.int32, a.shape, 1)
    b = jnp.where(lane < n, a, jnp.where(lane - n == row, 1.0, 0.0))
    for j in range(n - 1):
        factor = b[:, j : j + 1] * (1.0 / b[j : j + 1, j : j + 1])
        b = jnp.where(row > j, b - factor * b[j : j + 1, :], b)
    diag = jnp.sum(jnp.where(lane == row, b, 0.0), axis=1, keepdims=True)
    inv = pltpu.roll(b, 128 - n, 1) * (lax.rsqrt(diag) * scale)
    return inv[:, :n]


def kernel(pattern, class_weight, jac, row_class, probes, out, m, w, w16, qpad, yacc, zown,
           za_s, za_r, zc, ga, gb, gc, ys, y1, y2, load_sem,
           za_ss, za_rs, zc_ss, zc_rs, ga_ss, ga_rs, gb_ss, gb_rs, gc_ss, gc_rs,
           y1_ss, y1_rs, y2_ss, y2_rs):
    rows, params = lax.axis_index("rows"), lax.axis_index("params")
    y, zl = lax.rem(params, NY), lax.div(params, NY)
    core, zh, x = lax.rem(rows, 2), lax.rem(lax.div(rows, 2), 2), lax.div(rows, 4)
    group = m.shape[0] // NZ
    per = group // BLOCK
    scale = math.sqrt(P_SIZE)
    pending = []

    def yz_peer(dz, dy):
        return {"params": lax.rem(zl + dz, NZ) * NY + lax.rem(y + dy, NY)}

    def rows_peer(dx, dz, dc):
        return {"rows": lax.rem(x + dx, NX) * 4 + lax.rem(zh + dz, 2) * 2 + lax.rem(core + dc, 2)}

    yz_far = [(2, 2), (2, 1), (2, 3), (2, 0), (3, 2), (3, 1), (3, 3), (3, 0), (1, 2), (1, 1), (1, 3), (1, 0), (0, 2), (0, 1), (0, 3)]
    y1_far = [(0, 1, 1), (0, 1, 0), (0, 0, 1)]
    y2_far = [(2, 0, 1), (2, 0, 0), (1, 0, 1), (3, 0, 1), (1, 0, 0), (3, 0, 0), (0, 0, 1)]

    def send(src, dst, ssem, rsem, peer):
        copy = pltpu.make_async_remote_copy(
            src_ref=src, dst_ref=dst, send_sem=ssem, recv_sem=rsem, device_id=peer, device_id_type=MESH)
        copy.start()
        pending.append(copy)
        return copy

    loads = []
    for c in range(NZ):
        copy = pltpu.make_async_copy(
            jac.at[pl.ds(c * group, group), :], m.at[pl.ds(c * group, group), :], load_sem.at[c])
        copy.start()
        loads.append(copy)

    barrier = pltpu.get_barrier_semaphore()
    friends = [yz_peer(*d) for d in yz_far] + [rows_peer(*d) for d in y1_far + y2_far[:-1]]
    for peer in friends:
        pl.semaphore_signal(barrier, inc=1, device_id=peer, device_id_type=MESH)

    classes = row_class[...]
    weight = jnp.zeros(classes.shape, F32)
    for c in range(class_weight.shape[0]):
        weight = jnp.where(classes == c, class_weight[c], weight)
    w16[...] = weight
    for c in range(NZ):
        for i in range(per):
            w[c, :, i * BLOCK : (i + 1) * BLOCK] = w16[c * per + i : c * per + i + 1, :]
    qpad[...] = jnp.zeros_like(qpad)

    for c in range(NZ):
        loads[c].wait()
        for i in range(per):
            r = c * per + i
            for j in range(pattern.shape[1]):
                keep = jnp.full((BLOCK, BLOCK), pattern[r, j].astype(F32)).astype(BF16)
                at = (pl.ds(r * BLOCK, BLOCK), pl.ds(j * BLOCK, BLOCK))
                m[at] = m[at] * keep

    def rows_of(c):
        return m[pl.ds(pl.multiple_of(c * group, group), group), :]

    def raw_z(k, q, dz):
        part = dot_t(q, rows_of(lax.rem(zl + dz, NZ)))
        for i in range(NY):
            if dz:
                za_s[k, dz, i] = part[:, i * BLOCK : (i + 1) * BLOCK].astype(BF16)
            else:
                za_s[k, 0, i] = part[:, i * BLOCK : (i + 1) * BLOCK].astype(BF16)
                zown[i] = part[:, i * BLOCK : (i + 1) * BLOCK]

    def scatter_z(k, dz):
        copies = []
        for dy in (2, 1, 3, 0):
            if dz or dy:
                i = dz * NY + dy - 1
                copies.append(send(za_s.at[k, dz, lax.rem(y + dy, NY)], za_r.at[k, i],
                                   za_ss.at[k, i], za_rs.at[k, i], yz_peer(dz, dy)))
        return copies

    def gram(q):
        qpad[0:32, :] = q
        return pack_gram(dot_t(q, qpad[...]))

    def scatter_gram(k, q):
        ga[k, y] = gram(q)
        return [send(ga.at[k, y], ga.at[k, y], ga_ss.at[k, d - 1], ga_rs.at[k, d - 1], yz_peer(0, d))
                for d in (2, 1, 3)]

    def forward_gram(k, copies):
        for copy in copies:
            copy.wait_recv()
        gb[k, zl] = ((ga[k, 0] + ga[k, 1]) + ga[k, 2]) + ga[k, 3]
        return [send(gb.at[k, zl], gb.at[k, zl], gb_ss.at[k, d - 1], gb_rs.at[k, d - 1], yz_peer(d, 0))
                for d in (2, 3, 1)]

    def split_inverse(g):
        inv = scaled_inverse(g, scale)
        high = inv.astype(BF16)
        low = (inv - high.astype(F32)).astype(BF16)
        return jnp.concatenate([high, low], axis=0)

    def apply(inv2, v):
        u = dot(inv2, v)
        return u[:32] + u[32:]

    q = probes[...]
    for k in range(ITERS):
        a_copies = []
        if k == 0:
            for dz in (2, 3, 1, 0):
                raw_z(k, q, dz)
            pl.semaphore_wait(barrier, len(friends))
            for dz in (2, 3, 1, 0):
                a_copies += scatter_z(k, dz)
        else:
            for i, dz in enumerate((2, 3, 1, 0)):
                raw_z(k, q, dz)
                a_copies += scatter_z(k, dz)
                if i == 0:
                    g_copies = scatter_gram(k - 1, q)
            g_copies = forward_gram(k - 1, g_copies)
        total = zown[y]
        for copy in a_copies:
            copy.wait_recv()
        for i in range(NY * NZ - 1):
            total = total + za_r[k, i].astype(F32)
        zc[k, params] = total.astype(BF16)
        c_copies = {}
        for dz, dy in yz_far:
            i = dz * NY + dy - 1
            c_copies[dz, dy] = send(zc.at[k, params], zc.at[k, params], zc_ss.at[k, i], zc_rs.at[k, i], yz_peer(dz, dy))
        if k > 0:
            for copy in g_copies:
                copy.wait_recv()
            inv2 = split_inverse(((gb[k - 1, 0] + gb[k - 1, 1]) + gb[k - 1, 2]) + gb[k - 1, 3])
        acc = None
        for dz in (0, 1, 3, 2):
            c = lax.rem(zl + NZ - dz, NZ)
            for dy in range(NY):
                if dz or dy:
                    c_copies[dz, dy].wait_recv()
            z = jnp.concatenate([zc[k, c * NY + i] for i in range(NY)], axis=1)
            z = z.astype(F32) if k == 0 else apply(inv2, z)
            v = (z * w[c]).astype(BF16)
            part = dot(v, rows_of(c))
            acc = part if acc is None else acc + part
        yacc[0] = acc[:16]
        yacc[1] = acc[16:]
        mine = zh * 2 + core
        ys[k] = yacc[1 - core].astype(BF16)
        y1[k, mine] = yacc[core].astype(BF16)
        copies = []
        for i, (dx, dz, dc) in enumerate(y1_far):
            src = ys.at[k] if dc else y1.at[k, mine]
            copies.append(send(src, y1.at[k, mine], y1_ss.at[k, i], y1_rs.at[k, i], rows_peer(dx, dz, dc)))
        for copy in copies:
            copy.wait_recv()
        total = ((y1[k, 0].astype(F32) + y1[k, 1].astype(F32)) + y1[k, 2].astype(F32)) + y1[k, 3].astype(F32)
        y2[k, x, core] = total.astype(BF16)
        copies = [send(y2.at[k, x, core], y2.at[k, x, core], y2_ss.at[k, i], y2_rs.at[k, i], rows_peer(*d))
                  for i, d in enumerate(y2_far)]
        for copy in copies:
            copy.wait_recv()
        q = jnp.concatenate(
            [(((y2[k, 0, c].astype(F32) + y2[k, 1, c].astype(F32)) + y2[k, 2, c].astype(F32)) + y2[k, 3, c].astype(F32)).astype(BF16)
             for c in range(2)], axis=0)

    gc[params] = gram(q)
    copies = []
    for dz, dy in yz_far:
        i = dz * NY + dy - 1
        copies.append(send(gc.at[params], gc.at[params], gc_ss.at[i], gc_rs.at[i], yz_peer(dz, dy)))
    for copy in copies:
        copy.wait_recv()
    total = gc[0]
    for i in range(1, NY * NZ):
        total = total + gc[i]
    out[...] = apply(split_inverse(total), q).astype(BF16)
    for copy in pending:
        copy.wait_send()


def local(jacobian, pattern, row_class, class_weight, probes):
    nrows, ncols = jacobian.shape
    k, n = ITERS, NY * NZ
    vmem, dma = pltpu.VMEM, pltpu.SemaphoreType.DMA
    return pl.pallas_call(
        kernel,
        out_shape=jax.ShapeDtypeStruct(probes.shape, BF16),
        in_specs=[
            pl.BlockSpec(memory_space=pltpu.SMEM),
            pl.BlockSpec(memory_space=pltpu.SMEM),
            pl.BlockSpec(memory_space=pl.ANY),
            pl.BlockSpec(memory_space=pltpu.VMEM),
            pl.BlockSpec(memory_space=pltpu.VMEM),
        ],
        out_specs=pl.BlockSpec(memory_space=pltpu.VMEM),
        scratch_shapes=[
            vmem((nrows, ncols), BF16), vmem((NZ, 1, nrows // NZ), F32), vmem((nrows // 128, 128), F32),
            vmem((128, ncols), BF16), vmem((2, 16, ncols), F32), vmem((NY, 32, BLOCK), F32),
            vmem((k, NZ, NY, 32, BLOCK), BF16), vmem((k, n - 1, 32, BLOCK), BF16), vmem((k, n, 32, BLOCK), BF16),
            vmem((k - 1, NY, 8, 128), F32), vmem((k - 1, NZ, 8, 128), F32), vmem((n, 8, 128), F32),
            vmem((k, 16, ncols), BF16), vmem((k, 4, 16, ncols), BF16), vmem((k, NX, 2, 16, ncols), BF16),
            dma((NZ,)),
            dma((k, n - 1)), dma((k, n - 1)), dma((k, n - 1)), dma((k, n - 1)),
            dma((k - 1, 3)), dma((k - 1, 3)), dma((k - 1, 3)), dma((k - 1, 3)), dma((n - 1,)), dma((n - 1,)),
            dma((k, 3)), dma((k, 3)), dma((k, 7)), dma((k, 7)),
        ],
        compiler_params=pltpu.CompilerParams(collective_id=0, has_side_effects=True),
    )(pattern, class_weight, jacobian, row_class.reshape(-1, 128), probes)


def solution(mesh):
    placed = (P("rows", "params"), P("rows", "params"), P("rows"), P(), P(None, "params"))
    return jax.shard_map(
        local, mesh=mesh, in_specs=placed, out_specs=P(None, "params"), check_vma=False
    )
```

time: 120 us -> 112 us (0.933)
  Pallas kernels: 117 us -> 109 us
    pallas_call x1, Pallas kernels: 117 us -> 109 us  [local(): pl.pallas_call(kernel, out_shape=jax.ShapeDtypeStruct(probes.shape, BF16)...]
where the time goes in v2:
time: 112 us
  Pallas kernels  109 us (97%)
  local copies, waits for them, and re-layouts  2.78 us (2%)
    pallas_call x1, Pallas kernels, local(): pl.pallas_call(kernel, out_shape=jax.ShapeDtypeStruct(probes.shape, BF16)...  109 us
    unnamed x2, local copies, waits for them, and re-layouts  2.78 us

profile of v2, /device:TPU:1, one launch (start us, length us, event | category | flops | bytes accessed | tf_op | source)
XLA Modules:
  0.0 111.8 jit_solution(13042622526663021063)
XLA Ops:
  0.0 1.4 %copy.6.pattern = s32[16,6]{1,0:T(8,128)} copy(s32[16,6]{0,1:T(8,128)} %param.6) | data formatting | bytes 768 | tf_op args[1]
  1.4 109.0 %shard_map.55 = bf16[32,768]{1,0:T(8,128)(2,1)} custom-call(s32[16,6]{1,0:T(8,128)} %copy.6.pattern, f32[16]{0:T(128)} %class_weight.1, bf16[2048,768]{1,0:T(8,128)(2,1)} %jac.1, s32[16,128]{1,0:T(8,128)} %bitcast.1, bf16[32,768]{1,0:T(8,128)(2,1)} %probes.1), custom_call_target="tpu_custom_call" | custom-call | tf_op jit(solution)/shard_map/pallas_call | solution.py:233
  110.3 1.4 %copy.8 = bf16[32,768]{1,0:T(8,128)(2,1)} copy(bf16[32,768]{1,0:T(8,128)(2,1)} %shard_map.55) | data formatting | bytes 98304

commit v3 on v2

v3 whole, which is shorter than its diff:
```python
import functools
import math

import jax
import jax.numpy as jnp
from jax import lax
from jax.experimental import pallas as pl
from jax.experimental.pallas import tpu as pltpu
from jax.sharding import PartitionSpec as P

P_SIZE = 12288
BLOCK = 128
ITERS = 4
NY, NZ, NX = 4, 4, 4
MESH = pl.DeviceIdType.MESH
BF16, F32 = jnp.bfloat16, jnp.float32


def dot_t(a, b):
    return lax.dot_general(a, b, (((1,), (1,)), ((), ())), preferred_element_type=F32)


def dot(a, b):
    return jnp.dot(a, b, preferred_element_type=F32)


def pack_gram(g):
    return g[0:8] + pltpu.roll(g[8:16], 32, 1) + pltpu.roll(g[16:24], 64, 1) + pltpu.roll(g[24:32], 96, 1)


def scaled_inverse(gp, scale):
    a = jnp.concatenate([gp, pltpu.roll(gp, 96, 1), pltpu.roll(gp, 64, 1), pltpu.roll(gp, 32, 1)], axis=0)
    n = a.shape[0]
    row = lax.broadcasted_iota(jnp.int32, a.shape, 0)
    lane = lax.broadcasted_iota(jnp.int32, a.shape, 1)
    b = jnp.where(lane < n, a, jnp.where(lane - n == row, 1.0, 0.0))
    for j in range(n - 1):
        factor = b[:, j : j + 1] * (1.0 / b[j : j + 1, j : j + 1])
        b = jnp.where(row > j, b - factor * b[j : j + 1, :], b)
    diag = jnp.sum(jnp.where(lane == row, b, 0.0), axis=1, keepdims=True)
    inv = pltpu.roll(b, 128 - n, 1) * (lax.rsqrt(diag) * scale)
    return inv[:, :n]


def kernel(pattern_h, class_weight_h, jac, row_class_h, probes_h, out, pattern, class_weight, row_class, probes, m, w, w16, qpad, yacc, zown,
           za_s, za_r, zc, ga, gb, gc, ys, y1, y2, load_sem, in_sem,
           za_ss, za_rs, zc_ss, zc_rs, ga_ss, ga_rs, gb_ss, gb_rs, gc_ss, gc_rs,
           y1_ss, y1_rs, y2_ss, y2_rs):
    rows, params = lax.axis_index("rows"), lax.axis_index("params")
    y, zl = lax.rem(params, NY), lax.div(params, NY)
    core, zh, x = lax.rem(rows, 2), lax.rem(lax.div(rows, 2), 2), lax.div(rows, 4)
    group = m.shape[0] // NZ
    per = group // BLOCK
    scale = math.sqrt(P_SIZE)
    pending = []

    def yz_peer(dz, dy):
        return {"params": lax.rem(zl + dz, NZ) * NY + lax.rem(y + dy, NY)}

    def rows_peer(dx, dz, dc):
        return {"rows": lax.rem(x + dx, NX) * 4 + lax.rem(zh + dz, 2) * 2 + lax.rem(core + dc, 2)}

    def device(tz, ty):
        return {"params": tz * NY + ty}

    low = 1 - lax.div(zl, 2)
    z_order = [3 * low, 1 + low, zl + 1 - 2 * lax.rem(zl, 2), zl]
    y_order = [lax.rem(y + dy, NY) for dy in (2, 1, 3, 0)]
    others = [(tz, ty) for tz in z_order for ty in y_order][:-1]
    y1_far = [(0, 1, 1), (0, 1, 0), (0, 0, 1)]
    y2_far = [(2, 0, 1), (2, 0, 0), (1, 0, 1), (3, 0, 1), (1, 0, 0), (3, 0, 0), (0, 0, 1)]

    def send(src, dst, ssem, rsem, peer):
        copy = pltpu.make_async_remote_copy(
            src_ref=src, dst_ref=dst, send_sem=ssem, recv_sem=rsem, device_id=peer, device_id_type=MESH)
        copy.start()
        pending.append(copy)
        return copy

    inputs = [pltpu.make_async_copy(src, dst, in_sem.at[i]) for i, (src, dst) in enumerate(
        ((pattern_h, pattern), (probes_h, probes), (row_class_h, row_class), (class_weight_h, class_weight)))]
    loads = []
    for i, c in enumerate(z_order):
        at = pl.ds(pl.multiple_of(c * group, group), group)
        loads.append(pltpu.make_async_copy(jac.at[at, :], m.at[at, :], load_sem.at[i]))
    inputs[0].start()
    inputs[1].start()
    loads[0].start()
    inputs[2].start()
    inputs[3].start()
    for copy in loads[1:]:
        copy.start()

    barrier = pltpu.get_barrier_semaphore()
    friends = [device(*t) for t in others] + [rows_peer(*d) for d in y1_far + y2_far[:-1]]
    for peer in friends:
        pl.semaphore_signal(barrier, inc=1, device_id=peer, device_id_type=MESH)

    def prepare(i):
        loads[i].wait()
        c = z_order[i]
        for r in range(per):
            for j in range(pattern.shape[0]):
                keep = jnp.full((BLOCK, BLOCK), pattern[j, c * per + r].astype(F32)).astype(BF16)
                at = (pl.ds(pl.multiple_of(c * group + r * BLOCK, BLOCK), BLOCK), pl.ds(j * BLOCK, BLOCK))
                m[at] = m[at] * keep

    def weigh():
        inputs[2].wait()
        inputs[3].wait()
        classes = row_class[...]
        weight = jnp.zeros(classes.shape, F32)
        for c in range(class_weight.shape[0]):
            weight = jnp.where(classes == c, class_weight[c], weight)
        w16[...] = weight
        for c in range(NZ):
            for i in range(per):
                w[c, :, i * BLOCK : (i + 1) * BLOCK] = w16[c * per + i : c * per + i + 1, :]

    def rows_of(c):
        return m[pl.ds(pl.multiple_of(c * group, group), group), :]

    def raw_z(k, q, n):
        part = dot_t(q, rows_of(z_order[n]))
        for i in range(NY):
            block = part[:, i * BLOCK : (i + 1) * BLOCK]
            za_s[k, n, i] = block.astype(BF16)
            if n == NZ - 1:
                zown[i] = block

    def scatter_z(k, n):
        for i in range(n * NY, min((n + 1) * NY, len(others))):
            tz, ty = others[i]
            send(za_s.at[k, n, ty], za_r.at[k, params], za_ss.at[k, i], za_rs.at[k, params], device(tz, ty))

    def await_from(buf, sem, k, t):
        p = t[0] * NY + t[1]
        pltpu.make_async_remote_copy(
            src_ref=buf.at[k, p], dst_ref=buf.at[k, p], send_sem=sem.at[k, p], recv_sem=sem.at[k, p],
            device_id=device(*t), device_id_type=MESH).wait_recv()
        return p

    def gram(q):
        qpad[0:32, :] = q
        return pack_gram(dot_t(q, qpad[...]))

    def scatter_gram(k, q):
        ga[k, y] = gram(q)
        return [send(ga.at[k, y], ga.at[k, y], ga_ss.at[k, d - 1], ga_rs.at[k, d - 1], yz_peer(0, d))
                for d in (2, 1, 3)]

    def forward_gram(k, copies):
        for copy in copies:
            copy.wait_recv()
        gb[k, zl] = ((ga[k, 0] + ga[k, 1]) + ga[k, 2]) + ga[k, 3]
        return [send(gb.at[k, zl], gb.at[k, zl], gb_ss.at[k, d - 1], gb_rs.at[k, d - 1], yz_peer(d, 0))
                for d in (2, 3, 1)]

    def split_inverse(g):
        inv = scaled_inverse(g, scale)
        high = inv.astype(BF16)
        low = (inv - high.astype(F32)).astype(BF16)
        return jnp.concatenate([high, low], axis=0)

    def apply(inv2, v):
        u = dot(inv2, v)
        return u[:32] + u[32:]

    inputs[1].wait()
    inputs[0].wait()
    q = probes[...]
    for k in range(ITERS):
        for n in range(NZ):
            if k == 0:
                prepare(n)
            raw_z(k, q, n)
            if k == 0 and n == 0:
                pl.semaphore_wait(barrier, len(friends))
            scatter_z(k, n)
            if k > 0 and n == 0:
                g_copies = scatter_gram(k - 1, q)
        if k == 0:
            weigh()
            qpad[...] = jnp.zeros_like(qpad)
        else:
            g_copies = forward_gram(k - 1, g_copies)
        total = zown[y]
        for t in reversed(others):
            total = total + za_r[k, await_from(za_r, za_rs, k, t)].astype(F32)
        zc[k, params] = total.astype(BF16)
        for i, t in enumerate(others):
            send(zc.at[k, params], zc.at[k, params], zc_ss.at[k, i], zc_rs.at[k, params], device(*t))
        if k > 0:
            for copy in g_copies:
                copy.wait_recv()
            inv2 = split_inverse(((gb[k - 1, 0] + gb[k - 1, 1]) + gb[k - 1, 2]) + gb[k - 1, 3])
        acc = None
        for n in reversed(range(NZ)):
            c = z_order[n]
            for t in others[n * NY : (n + 1) * NY]:
                await_from(zc, zc_rs, k, t)
            z = jnp.concatenate([zc[k, c * NY + i] for i in range(NY)], axis=1)
            z = z.astype(F32) if k == 0 else apply(inv2, z)
            v = (z * w[c]).astype(BF16)
            part = dot(v, rows_of(c))
            acc = part if acc is None else acc + part
        yacc[0] = acc[:16]
        yacc[1] = acc[16:]
        mine = zh * 2 + core
        ys[k] = yacc[1 - core].astype(BF16)
        y1[k, mine] = yacc[core].astype(BF16)
        copies = []
        for i, (dx, dz, dc) in enumerate(y1_far):
            src = ys.at[k] if dc else y1.at[k, mine]
            copies.append(send(src, y1.at[k, mine], y1_ss.at[k, i], y1_rs.at[k, i], rows_peer(dx, dz, dc)))
        for copy in copies:
            copy.wait_recv()
        total = ((y1[k, 0].astype(F32) + y1[k, 1].astype(F32)) + y1[k, 2].astype(F32)) + y1[k, 3].astype(F32)
        y2[k, x, core] = total.astype(BF16)
        copies = [send(y2.at[k, x, core], y2.at[k, x, core], y2_ss.at[k, i], y2_rs.at[k, i], rows_peer(*d))
                  for i, d in enumerate(y2_far)]
        for copy in copies:
            copy.wait_recv()
        q = jnp.concatenate(
            [(((y2[k, 0, c].astype(F32) + y2[k, 1, c].astype(F32)) + y2[k, 2, c].astype(F32)) + y2[k, 3, c].astype(F32)).astype(BF16)
             for c in range(2)], axis=0)

    gc[0, params] = gram(q)
    for i, t in enumerate(others):
        send(gc.at[0, params], gc.at[0, params], gc_ss.at[i], gc_rs.at[0, params], device(*t))
    for t in others:
        await_from(gc, gc_rs, 0, t)
    total = gc[0, 0]
    for i in range(1, NY * NZ):
        total = total + gc[0, i]
    out[...] = apply(split_inverse(total), q).astype(BF16)
    for copy in pending:
        copy.wait_send()


def local(jacobian, pattern, row_class, class_weight, probes):
    nrows, ncols = jacobian.shape
    k, n = ITERS, NY * NZ
    vmem, dma = pltpu.VMEM, pltpu.SemaphoreType.DMA
    return pl.pallas_call(
        kernel,
        out_shape=jax.ShapeDtypeStruct(probes.shape, BF16),
        in_specs=[pl.BlockSpec(memory_space=pl.ANY)] * 5,
        out_specs=pl.BlockSpec(memory_space=pltpu.VMEM),
        scratch_shapes=[
            pltpu.SMEM(pattern.shape[::-1], jnp.int32), pltpu.SMEM(class_weight.shape, F32),
            vmem((nrows // 128, 128), jnp.int32), vmem(probes.shape, BF16),
            vmem((nrows, ncols), BF16), vmem((NZ, 1, nrows // NZ), F32), vmem((nrows // 128, 128), F32),
            vmem((128, ncols), BF16), vmem((2, 16, ncols), F32), vmem((NY, 32, BLOCK), F32),
            vmem((k, NZ, NY, 32, BLOCK), BF16), vmem((k, n, 32, BLOCK), BF16), vmem((k, n, 32, BLOCK), BF16),
            vmem((k - 1, NY, 8, 128), F32), vmem((k - 1, NZ, 8, 128), F32), vmem((1, n, 8, 128), F32),
            vmem((k, 16, ncols), BF16), vmem((k, 4, 16, ncols), BF16), vmem((k, NX, 2, 16, ncols), BF16),
            dma((NZ,)), dma((4,)),
            dma((k, n - 1)), dma((k, n)), dma((k, n - 1)), dma((k, n)),
            dma((k - 1, 3)), dma((k - 1, 3)), dma((k - 1, 3)), dma((k - 1, 3)), dma((n - 1,)), dma((1, n)),
            dma((k, 3)), dma((k, 3)), dma((k, 7)), dma((k, 7)),
        ],
        compiler_params=pltpu.CompilerParams(collective_id=0, has_side_effects=True),
    )(pattern.T, class_weight, jacobian, row_class.reshape(-1, 128), probes)


def solution(mesh):
    placed = (P("rows", "params"), P("rows", "params"), P("rows"), P(), P(None, "params"))
    return jax.shard_map(
        local, mesh=mesh, in_specs=placed, out_specs=P(None, "params"), check_vma=False
    )
```

time: 112 us -> 108 us (0.964)
  Pallas kernels: 109 us -> 106 us
  local copies, waits for them, and re-layouts: 2.78 us -> 1.42 us
    pallas_call x1, Pallas kernels: 109 us -> 106 us  [local(): pl.pallas_call(kernel, out_shape=jax.ShapeDtypeStruct(probes.shape, BF16)...]
    unnamed x2 -> x1, local copies, waits for them, and re-layouts: 2.78 us -> 1.42 us
where the time goes in v3:
time: 108 us; the launch traced here: 107 us
  Pallas kernels  106 us (98%)
  local copies, waits for them, and re-layouts  1.42 us (1%)
    pallas_call x1, Pallas kernels, local(): pl.pallas_call(kernel, out_shape=jax.ShapeDtypeStruct(probes.shape, BF16)...  106 us

profile of v3, /device:TPU:1, one launch (start us, length us, event | category | flops | bytes accessed | tf_op | source)
XLA Modules:
  0.0 107.4 jit_solution(183675470693903543)
XLA Ops:
  0.0 106.0 %shard_map.55 = bf16[32,768]{1,0:T(8,128)(2,1)} custom-call(s32[6,16]{1,0:T(8,128)} %bitcast.3, f32[16]{0:T(128)} %class_weight_h.1, bf16[2048,768]{1,0:T(8,128)(2,1)} %jac.1, s32[16,128]{1,0:T(8,128)} %bitcast.2, bf16[32,768]{1,0:T(8,128)(2,1)} %probes_h.1), custom_call_target="tpu_custom_call" | custom-call | tf_op jit(solution)/shard_map/pallas_call | solution.py:245
  106.0 1.4 %copy.7 = bf16[32,768]{1,0:T(8,128)(2,1)} copy(bf16[32,768]{1,0:T(8,128)(2,1)} %shard_map.55) | data formatting | bytes 98304

commit v4 on v3

--- a/solution.py
+++ b/solution.py
@@ -22,6 +22,13 @@
 
 def dot(a, b):
     return jnp.dot(a, b, preferred_element_type=F32)
+
+
+def add_all(terms):
+    total = terms[0].astype(F32)
+    for term in terms[1:]:
+        total = total + term.astype(F32)
+    return total
 
 
 def pack_gram(g):
@@ -42,15 +49,16 @@
     return inv[:, :n]
 
 
-def kernel(pattern_h, class_weight_h, jac, row_class_h, probes_h, out, pattern, class_weight, row_class, probes, m, w, w16, qpad, yacc, zown,
-           za_s, za_r, zc, ga, gb, gc, ys, y1, y2, load_sem, in_sem,
+def kernel(pattern_h, class_weight_h, jac, row_class_h, probes_h, out, pattern, class_weight, row_class, probes, m, w, w16, qpad, zown,
+           za_s, za_r, zc, ga, gb, gc, yp, a1, a2, b1, b2, load_sem, in_sem,
            za_ss, za_rs, zc_ss, zc_rs, ga_ss, ga_rs, gb_ss, gb_rs, gc_ss, gc_rs,
-           y1_ss, y1_rs, y2_ss, y2_rs):
+           a1_ss, a1_rs, a2_ss, a2_rs, b1_ss, b1_rs, b2_ss, b2_rs):
     rows, params = lax.axis_index("rows"), lax.axis_index("params")
     y, zl = lax.rem(params, NY), lax.div(params, NY)
     core, zh, x = lax.rem(rows, 2), lax.rem(lax.div(rows, 2), 2), lax.div(rows, 4)
     group = m.shape[0] // NZ
     per = group // BLOCK
+    half = m.shape[1] // 2
     scale = math.sqrt(P_SIZE)
     pending = []
 
@@ -67,8 +75,8 @@
     z_order = [3 * low, 1 + low, zl + 1 - 2 * lax.rem(zl, 2), zl]
     y_order = [lax.rem(y + dy, NY) for dy in (2, 1, 3, 0)]
     others = [(tz, ty) for tz in z_order for ty in y_order][:-1]
-    y1_far = [(0, 1, 1), (0, 1, 0), (0, 0, 1)]
-    y2_far = [(2, 0, 1), (2, 0, 0), (1, 0, 1), (3, 0, 1), (1, 0, 0), (3, 0, 0), (0, 0, 1)]
+    z_far = [(0, 1, 1), (0, 1, 0), (0, 0, 1)]
+    x_far = [(2, 0, 1), (2, 0, 0), (1, 0, 1), (3, 0, 1), (1, 0, 0), (3, 0, 0), (0, 0, 1)]
 
     def send(src, dst, ssem, rsem, peer):
         copy = pltpu.make_async_remote_copy(
@@ -92,7 +100,7 @@
         copy.start()
 
     barrier = pltpu.get_barrier_semaphore()
-    friends = [device(*t) for t in others] + [rows_peer(*d) for d in y1_far + y2_far[:-1]]
+    friends = [device(*t) for t in others] + [rows_peer(*d) for d in z_far + x_far[:-1]]
     for peer in friends:
         pl.semaphore_signal(barrier, inc=1, device_id=peer, device_id_type=MESH)
 
@@ -204,26 +212,33 @@
             v = (z * w[c]).astype(BF16)
             part = dot(v, rows_of(c))
             acc = part if acc is None else acc + part
-        yacc[0] = acc[:16]
-        yacc[1] = acc[16:]
-        mine = zh * 2 + core
-        ys[k] = yacc[1 - core].astype(BF16)
-        y1[k, mine] = yacc[core].astype(BF16)
-        copies = []
-        for i, (dx, dz, dc) in enumerate(y1_far):
-            src = ys.at[k] if dc else y1.at[k, mine]
-            copies.append(send(src, y1.at[k, mine], y1_ss.at[k, i], y1_rs.at[k, i], rows_peer(dx, dz, dc)))
-        for copy in copies:
-            copy.wait_recv()
-        total = ((y1[k, 0].astype(F32) + y1[k, 1].astype(F32)) + y1[k, 2].astype(F32)) + y1[k, 3].astype(F32)
-        y2[k, x, core] = total.astype(BF16)
-        copies = [send(y2.at[k, x, core], y2.at[k, x, core], y2_ss.at[k, i], y2_rs.at[k, i], rows_peer(*d))
-                  for i, d in enumerate(y2_far)]
-        for copy in copies:
-            copy.wait_recv()
-        q = jnp.concatenate(
-            [(((y2[k, 0, c].astype(F32) + y2[k, 1, c].astype(F32)) + y2[k, 2, c].astype(F32)) + y2[k, 3, c].astype(F32)).astype(BF16)
-             for c in range(2)], axis=0)
+        for h in range(2):
+            for f in range(2):
+                yp[k, h, f] = acc[16 * h : 16 * h + 16, half * f : half * f + half].astype(BF16)
+        za, xa = zh * 2 + core, x * 2 + core
+        a1[k, za] = yp[k, core, 0]
+        b1[k, xa] = yp[k, core, 1]
+
+        def exchange(far, source, dst, ss, rs):
+            return [send(source(d[2]), dst, ss.at[k, i], rs.at[k, i], rows_peer(*d)) for i, d in enumerate(far)]
+
+        a_copies = exchange(z_far, lambda dc: yp.at[k, lax.rem(core + dc, 2), 0], a1.at[k, za], a1_ss, a1_rs)
+        b_copies = exchange(x_far, lambda dc: yp.at[k, lax.rem(core + dc, 2), 1], b1.at[k, xa], b1_ss, b1_rs)
+        for copy in b_copies:
+            copy.wait_recv()
+        b2[k, za] = add_all([b1[k, i] for i in range(2 * NX)]).astype(BF16)
+        b_copies = exchange(z_far, lambda dc: b2.at[k, za], b2.at[k, za], b2_ss, b2_rs)
+        for copy in a_copies:
+            copy.wait_recv()
+        a2[k, xa] = add_all([a1[k, i] for i in range(4)]).astype(BF16)
+        a_copies = exchange(x_far, lambda dc: a2.at[k, xa], a2.at[k, xa], a2_ss, a2_rs)
+        for copy in a_copies + b_copies:
+            copy.wait_recv()
+        q = jnp.concatenate([
+            jnp.concatenate([
+                add_all([a2[k, i * 2 + c] for i in range(NX)]).astype(BF16),
+                add_all([b2[k, i * 2 + c] for i in range(2)]).astype(BF16)], axis=1)
+            for c in range(2)], axis=0)
 
     gc[0, params] = gram(q)
     for i, t in enumerate(others):
@@ -240,7 +255,7 @@
 
 def local(jacobian, pattern, row_class, class_weight, probes):
     nrows, ncols = jacobian.shape
-    k, n = ITERS, NY * NZ
+    k, n, half = ITERS, NY * NZ, ncols // 2
     vmem, dma = pltpu.VMEM, pltpu.SemaphoreType.DMA
     return pl.pallas_call(
         kernel,
@@ -251,17 +266,19 @@
             pltpu.SMEM(pattern.shape[::-1], jnp.int32), pltpu.SMEM(class_weight.shape, F32),
             vmem((nrows // 128, 128), jnp.int32), vmem(probes.shape, BF16),
             vmem((nrows, ncols), BF16), vmem((NZ, 1, nrows // NZ), F32), vmem((nrows // 128, 128), F32),
-            vmem((128, ncols), BF16), vmem((2, 16, ncols), F32), vmem((NY, 32, BLOCK), F32),
+            vmem((128, ncols), BF16), vmem((NY, 32, BLOCK), F32),
             vmem((k, NZ, NY, 32, BLOCK), BF16), vmem((k, n, 32, BLOCK), BF16), vmem((k, n, 32, BLOCK), BF16),
             vmem((k - 1, NY, 8, 128), F32), vmem((k - 1, NZ, 8, 128), F32), vmem((1, n, 8, 128), F32),
-            vmem((k, 16, ncols), BF16), vmem((k, 4, 16, ncols), BF16), vmem((k, NX, 2, 16, ncols), BF16),
+            vmem((k, 2, 2, 16, half), BF16), vmem((k, 4, 16, half), BF16), vmem((k, 2 * NX, 16, half), BF16),
+            vmem((k, 2 * NX, 16, half), BF16), vmem((k, 4, 16, half), BF16),
             dma((NZ,)), dma((4,)),
             dma((k, n - 1)), dma((k, n)), dma((k, n - 1)), dma((k, n)),
             dma((k - 1, 3)), dma((k - 1, 3)), dma((k - 1, 3)), dma((k - 1, 3)), dma((n - 1,)), dma((1, n)),
-            dma((k, 3)), dma((k, 3)), dma((k, 7)), dma((k, 7)),
+            dma((k, 3)), dma((k, 3)), dma((k, 7)), dma((k, 7)), dma((k, 7)), dma((k, 7)), dma((k, 3)), dma((k, 3)),
         ],
-        compiler_params=pltpu.CompilerParams(collective_id=0, has_side_effects=True),
-    )(pattern.T, class_weight, jacobian, row_class.reshape(-1, 128), probes)
+        compiler_params=pltpu.CompilerParams(collective_id=0, has_side_effects=True, vmem_limit_bytes=32 * 2**20),
+    )(*(pltpu.with_memory_space_constraint(a, pltpu.HBM)
+        for a in (pattern.T, class_weight, jacobian, row_class.reshape(-1, 128), probes)))
 
 
 def solution(mesh):

time: 108 us -> 104 us (0.963)
  Pallas kernels: 106 us -> 104 us
    pallas_call x1, Pallas kernels: 106 us -> 104 us  [local(): pl.pallas_call(kernel, out_shape=jax.ShapeDtypeStruct(probes.shape, BF16)...]
where the time goes in v4:
time: 104 us
  Pallas kernels  104 us (100%)
    pallas_call x1, Pallas kernels, local(): pl.pallas_call(kernel, out_shape=jax.ShapeDtypeStruct(probes.shape, BF16)...  104 us

profile of v4, /device:TPU:1, one launch (start us, length us, event | category | flops | bytes accessed | tf_op | source)
XLA Modules:
  0.0 104.4 jit_solution(4701037845451491204)
XLA Ops:
  0.0 103.7 %shard_map.55 = bf16[32,768]{1,0:T(8,128)(2,1)S(1)} custom-call(s32[6,16]{1,0:T(8,128)} %bitcast.3, f32[16]{0:T(128)} %class_weight_h.1, bf16[2048,768]{1,0:T(8,128)(2,1)} %jac.1, s32[16,128]{1,0:T(8,128)} %bitcast.2, bf16[32,768]{1,0:T(8,128)(2,1)} %probes_h.1), custom_call_target="tpu_custom_call" | custom-call | tf_op jit(solution)/shard_map/pallas_call | solution.py:260
  103.7 0.6 copy.7

commit v5 on v4

--- a/solution.py
+++ b/solution.py
@@ -36,17 +36,41 @@
 
 
 def scaled_inverse(gp, scale):
-    a = jnp.concatenate([gp, pltpu.roll(gp, 96, 1), pltpu.roll(gp, 64, 1), pltpu.roll(gp, 32, 1)], axis=0)
-    n = a.shape[0]
-    row = lax.broadcasted_iota(jnp.int32, a.shape, 0)
-    lane = lax.broadcasted_iota(jnp.int32, a.shape, 1)
-    b = jnp.where(lane < n, a, jnp.where(lane - n == row, 1.0, 0.0))
-    for j in range(n - 1):
-        factor = b[:, j : j + 1] * (1.0 / b[j : j + 1, j : j + 1])
-        b = jnp.where(row > j, b - factor * b[j : j + 1, :], b)
-    diag = jnp.sum(jnp.where(lane == row, b, 0.0), axis=1, keepdims=True)
-    inv = pltpu.roll(b, 128 - n, 1) * (lax.rsqrt(diag) * scale)
-    return inv[:, :n]
+    tile = gp.shape
+    row = lax.broadcasted_iota(jnp.int32, tile, 0)
+    lane = lax.broadcasted_iota(jnp.int32, tile, 1)
+    nb, n = 4, 32
+    b = []
+    for i in range(nb):
+        a = pltpu.roll(gp, 128 - 32 * i, 1) if i else gp
+        b.append(jnp.where(lane < n, a, jnp.where(lane - n == row + 8 * i, 1.0, 0.0)))
+
+    def spread(v):
+        return jnp.broadcast_to(v, tile)
+
+    for g in range(nb):
+        col = {i: [spread(b[i][:, 8 * g + k : 8 * g + k + 1]) for k in range(8)] for i in range(g, nb)}
+        r = [spread(b[g][m : m + 1, :]) for m in range(8)]
+        a = {(m, k): spread(col[g][k][m : m + 1, :]) for m in range(8) for k in range(m + 1)}
+        for k in range(8):
+            inv = 1.0 / a[k, k]
+            for i in range(g + 1, nb):
+                factor = col[i][k] * inv
+                b[i] = b[i] - factor * r[k]
+                for m in range(k + 1, 8):
+                    col[i][m] = col[i][m] - factor * a[m, k]
+            for m in range(k + 1, 8):
+                factor = a[m, k] * inv
+                r[m] = r[m] - factor * r[k]
+                for l in range(k + 1, m + 1):
+                    a[m, l] = a[m, l] - factor * a[l, k]
+        for m in range(8):
+            b[g] = jnp.where(row == m, r[m], b[g])
+    out = []
+    for i in range(nb):
+        diag = jnp.sum(jnp.where(lane == row + 8 * i, b[i], 0.0), axis=1, keepdims=True)
+        out.append(pltpu.roll(b[i], 128 - n, 1) * (lax.rsqrt(diag) * scale))
+    return jnp.concatenate(out, axis=0)[:, :n]
 
 
 def kernel(pattern_h, class_weight_h, jac, row_class_h, probes_h, out, pattern, class_weight, row_class, probes, m, w, w16, qpad, zown,
@@ -243,13 +267,15 @@
     gc[0, params] = gram(q)
     for i, t in enumerate(others):
         send(gc.at[0, params], gc.at[0, params], gc_ss.at[i], gc_rs.at[0, params], device(*t))
+    for copy in pending[: -len(others)]:
+        copy.wait_send()
     for t in others:
         await_from(gc, gc_rs, 0, t)
     total = gc[0, 0]
     for i in range(1, NY * NZ):
         total = total + gc[0, i]
     out[...] = apply(split_inverse(total), q).astype(BF16)
-    for copy in pending:
+    for copy in pending[-len(others) :]:
         copy.wait_send()
 
 

time: 104 us -> 102 us (0.981)
  Pallas kernels: 104 us -> 101 us
    pallas_call x1, Pallas kernels: 104 us -> 101 us  [local(): pl.pallas_call(kernel, out_shape=jax.ShapeDtypeStruct(probes.shape, BF16)...]
where the time goes in v5:
time: 102 us; the launch traced here: 101 us
  Pallas kernels  101 us (99%)
    pallas_call x1, Pallas kernels, local(): pl.pallas_call(kernel, out_shape=jax.ShapeDtypeStruct(probes.shape, BF16)...  101 us

profile of v5, /device:TPU:1, one launch (start us, length us, event | category | flops | bytes accessed | tf_op | source)
XLA Modules:
  0.0 101.4 jit_solution(390133102555053353)
XLA Ops:
  0.0 100.8 %shard_map.55 = bf16[32,768]{1,0:T(8,128)(2,1)S(1)} custom-call(s32[6,16]{1,0:T(8,128)} %bitcast.3, f32[16]{0:T(128)} %class_weight_h.1, bf16[2048,768]{1,0:T(8,128)(2,1)} %jac.1, s32[16,128]{1,0:T(8,128)} %bitcast.2, bf16[32,768]{1,0:T(8,128)(2,1)} %probes_h.1), custom_call_target="tpu_custom_call" | custom-call | tf_op jit(solution)/shard_map/pallas_call | solution.py:286
  100.8 0.6 copy.7

commit v6 on v5

--- a/solution.py
+++ b/solution.py
@@ -80,9 +80,9 @@
     rows, params = lax.axis_index("rows"), lax.axis_index("params")
     y, zl = lax.rem(params, NY), lax.div(params, NY)
     core, zh, x = lax.rem(rows, 2), lax.rem(lax.div(rows, 2), 2), lax.div(rows, 4)
-    group = m.shape[0] // NZ
+    group = m.shape[1]
     per = group // BLOCK
-    half = m.shape[1] // 2
+    half = m.shape[2] // 2
     scale = math.sqrt(P_SIZE)
     pending = []
 
@@ -114,7 +114,7 @@
     loads = []
     for i, c in enumerate(z_order):
         at = pl.ds(pl.multiple_of(c * group, group), group)
-        loads.append(pltpu.make_async_copy(jac.at[at, :], m.at[at, :], load_sem.at[i]))
+        loads.append(pltpu.make_async_copy(jac.at[at, :], m.at[i], load_sem.at[i]))
     inputs[0].start()
     inputs[1].start()
     loads[0].start()
@@ -129,12 +129,11 @@
         pl.semaphore_signal(barrier, inc=1, device_id=peer, device_id_type=MESH)
 
     def prepare(i):
-        loads[i].wait()
         c = z_order[i]
         for r in range(per):
             for j in range(pattern.shape[0]):
                 keep = jnp.full((BLOCK, BLOCK), pattern[j, c * per + r].astype(F32)).astype(BF16)
-                at = (pl.ds(pl.multiple_of(c * group + r * BLOCK, BLOCK), BLOCK), pl.ds(j * BLOCK, BLOCK))
+                at = (i, pl.ds(r * BLOCK, BLOCK), pl.ds(j * BLOCK, BLOCK))
                 m[at] = m[at] * keep
 
     def weigh():
@@ -149,11 +148,8 @@
             for i in range(per):
                 w[c, :, i * BLOCK : (i + 1) * BLOCK] = w16[c * per + i : c * per + i + 1, :]
 
-    def rows_of(c):
-        return m[pl.ds(pl.multiple_of(c * group, group), group), :]
-
     def raw_z(k, q, n):
-        part = dot_t(q, rows_of(z_order[n]))
+        part = dot_t(q, m[n])
         for i in range(NY):
             block = part[:, i * BLOCK : (i + 1) * BLOCK]
             za_s[k, n, i] = block.astype(BF16)
@@ -202,14 +198,22 @@
     inputs[0].wait()
     q = probes[...]
     for k in range(ITERS):
+        if k == 0:
+            loads[0].wait()
+            prepare(0)
         for n in range(NZ):
-            if k == 0:
-                prepare(n)
+            if k == 0 and n < NZ - 1:
+                loads[n + 1].wait()
             raw_z(k, q, n)
-            if k == 0 and n == 0:
+            if k == 0 and n < NZ - 1:
+                prepare(n + 1)
+            if k == 0 and n == NZ - 1:
                 pl.semaphore_wait(barrier, len(friends))
-            scatter_z(k, n)
-            if k > 0 and n == 0:
+                for i in range(NZ):
+                    scatter_z(k, i)
+            if k > 0:
+                scatter_z(k, n)
+            if k > 0 and n == 1:
                 g_copies = scatter_gram(k - 1, q)
         if k == 0:
             weigh()
@@ -234,7 +238,7 @@
             z = jnp.concatenate([zc[k, c * NY + i] for i in range(NY)], axis=1)
             z = z.astype(F32) if k == 0 else apply(inv2, z)
             v = (z * w[c]).astype(BF16)
-            part = dot(v, rows_of(c))
+            part = dot(v, m[n])
             acc = part if acc is None else acc + part
         for h in range(2):
             for f in range(2):
@@ -291,7 +295,7 @@
         scratch_shapes=[
             pltpu.SMEM(pattern.shape[::-1], jnp.int32), pltpu.SMEM(class_weight.shape, F32),
             vmem((nrows // 128, 128), jnp.int32), vmem(probes.shape, BF16),
-            vmem((nrows, ncols), BF16), vmem((NZ, 1, nrows // NZ), F32), vmem((nrows // 128, 128), F32),
+            vmem((NZ, nrows // NZ, ncols), BF16), vmem((NZ, 1, nrows // NZ), F32), vmem((nrows // 128, 128), F32),
             vmem((128, ncols), BF16), vmem((NY, 32, BLOCK), F32),
             vmem((k, NZ, NY, 32, BLOCK), BF16), vmem((k, n, 32, BLOCK), BF16), vmem((k, n, 32, BLOCK), BF16),
             vmem((k - 1, NY, 8, 128), F32), vmem((k - 1, NZ, 8, 128), F32), vmem((1, n, 8, 128), F32),

time: 102 us -> 101 us (level)
  no operation moved by 1% of the time
where the time goes in v6:
time: 101 us
  Pallas kernels  101 us (100%)
    pallas_call x1, Pallas kernels, local(): pl.pallas_call(kernel, out_shape=jax.ShapeDtypeStruct(probes.shape, BF16)...  101 us

profile of v6, /device:TPU:1, one launch (start us, length us, event | category | flops | bytes accessed | tf_op | source)
XLA Modules:
  0.0 101.4 jit_solution(15895390419242646117)
XLA Ops:
  0.0 100.7 %shard_map.55 = bf16[32,768]{1,0:T(8,128)(2,1)S(1)} custom-call(s32[6,16]{1,0:T(8,128)} %bitcast.3, f32[16]{0:T(128)} %class_weight_h.1, bf16[2048,768]{1,0:T(8,128)(2,1)} %jac.1, s32[16,128]{1,0:T(8,128)} %bitcast.2, bf16[32,768]{1,0:T(8,128)(2,1)} %probes_h.1), custom_call_target="tpu_custom_call" | custom-call | tf_op jit(solution)/shard_map/pallas_call | solution.py:290
  100.7 0.6 copy.7

commit v7 on v6

--- a/solution.py
+++ b/solution.py
@@ -213,7 +213,7 @@
                     scatter_z(k, i)
             if k > 0:
                 scatter_z(k, n)
-            if k > 0 and n == 1:
+            if k > 0 and n == NZ - 1:
                 g_copies = scatter_gram(k - 1, q)
         if k == 0:
             weigh()
@@ -224,7 +224,8 @@
         for t in reversed(others):
             total = total + za_r[k, await_from(za_r, za_rs, k, t)].astype(F32)
         zc[k, params] = total.astype(BF16)
-        for i, t in enumerate(others):
+        for i in (0, 1, 2, 4, 5, 6, 8, 3, 9, 10, 7, 12, 11, 13, 14):
+            t = others[i]
             send(zc.at[k, params], zc.at[k, params], zc_ss.at[k, i], zc_rs.at[k, params], device(*t))
         if k > 0:
             for copy in g_copies:

time: 101 us -> 101 us (level)
  Pallas kernels: 101 us -> 99.9 us
where the time goes in v7:
time: 101 us
  Pallas kernels  99.9 us (99%)
    pallas_call x1, Pallas kernels, local(): pl.pallas_call(kernel, out_shape=jax.ShapeDtypeStruct(probes.shape, BF16)...  99.9 us

profile of v7, /device:TPU:1, one launch (start us, length us, event | category | flops | bytes accessed | tf_op | source)
XLA Modules:
  0.0 100.6 jit_solution(10784261130545328712)
XLA Ops:
  0.0 99.9 %shard_map.55 = bf16[32,768]{1,0:T(8,128)(2,1)S(1)} custom-call(s32[6,16]{1,0:T(8,128)} %bitcast.3, f32[16]{0:T(128)} %class_weight_h.1, bf16[2048,768]{1,0:T(8,128)(2,1)} %jac.1, s32[16,128]{1,0:T(8,128)} %bitcast.2, bf16[32,768]{1,0:T(8,128)(2,1)} %probes_h.1), custom_call_target="tpu_custom_call" | custom-call | tf_op jit(solution)/shard_map/pallas_call | solution.py:291
  99.9 0.6 copy.7
